TPU v7x, 32 devices: a whole 2x2x4 slice. The times are simulated.
32 devices in a mesh: dp: 8 (over y, x, core), mp: 4 (over z).
Axes of the slice: x: 2, y: 2, z: 4, core: 2. Of those that a mesh axis runs over, the one named last changes fastest.
Arguments:
- patches: bfloat16 [1024, 6144], P('dp', 'mp'), may hold values from -64 to 64
- send_start: int32 [8, 8], P('dp'), may hold values from 0 to 128, as said below
- run_length: int32 [8, 8], P('dp'), may hold values from 0 to 32, as said below
- slot_start: int32 [8, 8], P('dp'), may hold values from 0 to 128, as said below
- image_ids: int32 [8, 128], P('dp'), may hold values from 0 to 7, never falling along the last dimension, each value on 1 to 32 neighbouring positions
- norm_gain: float32 [6144], replicated, may hold values from 0.1 to 1.9
- qkv_weight: bfloat16 [6144, 3, 4096], P('dp', None, 'mp'), may hold values from -0.078125 to 0.078125
- query_gain: float32 [128], replicated, may hold values from 0.1 to 1.9
- key_gain: float32 [128], replicated, may hold values from 0.1 to 1.9
- out_weight: bfloat16 [4096, 6144], P('mp'), may hold values from -0.09375 to 0.09375
Outputs:
- packed: bfloat16 [1024, 6144], P('dp', 'mp')
- attended: bfloat16 [1024, 6144], P('dp', 'mp')
Inputs may be any that keep to these rules, and one draw needn't show every extreme that they name: `run_length`: every source's runs sum to 128 and every pack's runs sum to 128; the longest run is exactly 32. `send_start`: the runs of one source device do not intersect and cover its 128 rows. `slot_start`: the runs into one pack do not intersect and fill its 128 slots. `image_ids`: image numbers never fall along a pack; equal numbers mark one image.
All inputs are finite; a program needn't handle non-finite values.
Results may differ from a plain program's by a relative error of at most 0.011.
Values may be sent and summed in bfloat16 or wider, within the bound.
A program may use at most 128 MiB of HBM per device.

v0:
```python
import jax
import jax.numpy as jnp
from jax import lax
from jax.sharding import PartitionSpec as P

epsilon = 1e-06


def row_norm(values, scales):
    middle = jnp.mean(values, axis=-1, keepdims=True)
    spread = jnp.mean(values * values, axis=-1, keepdims=True) - middle * middle
    return (values - middle) * lax.rsqrt(spread + epsilon) * scales


def on_device(
    patches,
    send_start,
    run_length,
    slot_start,
    image_ids,
    norm_gain,
    qkv_weight,
    query_gain,
    key_gain,
    out_weight,
):
    pack_rows, feat_local = patches.shape
    pack_count = lax.axis_size("dp")
    mp_count = lax.axis_size("mp")
    capacity = 2 * pack_rows // pack_count
    local_cols = qkv_weight.shape[1] * qkv_weight.shape[2]
    offsets = jnp.arange(capacity, dtype=jnp.int32)
    rows = jnp.arange(pack_rows, dtype=jnp.int32)
    x = patches.astype(jnp.float32)
    sums = jnp.stack([jnp.sum(x, axis=-1), jnp.sum(x * x, axis=-1)])
    sums = lax.psum(sums, "mp") / (feat_local * mp_count)
    middle = sums[0][:, None]
    spread = sums[1][:, None] - middle * middle
    gain = lax.dynamic_slice_in_dim(norm_gain, lax.axis_index("mp") * feat_local, feat_local)
    normed = ((x - middle) * lax.rsqrt(spread + epsilon) * gain).astype(jnp.bfloat16)
    wide = lax.all_gather(normed, "mp", axis=1, tiled=True)
    slices = lax.all_to_all(wide, "dp", split_axis=1, concat_axis=0, tiled=True)
    tables = jnp.concatenate([send_start, run_length, slot_start], axis=0)[None]
    tables = lax.all_gather(tables, "dp", axis=0, tiled=True)
    starts, lengths, slots = (tables[:, 0].T, tables[:, 1].T, tables[:, 2])
    inside = (rows >= slots[:, :, None]) & (rows < (slots + lengths)[:, :, None])
    base = jnp.arange(pack_count, dtype=jnp.int32)[None, :] * pack_rows + starts - slots
    origin = jnp.sum(jnp.where(inside, base[:, :, None] + rows, 0), axis=1).reshape(-1)
    chosen = (origin[:, None] == jnp.arange(origin.shape[0], dtype=jnp.int32)).astype(jnp.bfloat16)
    ordered = jnp.dot(chosen, slices, preferred_element_type=jnp.float32).astype(jnp.bfloat16)
    partial = jnp.dot(
        ordered,
        qkv_weight.reshape(qkv_weight.shape[0], local_cols),
        preferred_element_type=jnp.float32,
    ).astype(jnp.bfloat16)
    projected = lax.psum_scatter(partial, "dp", scatter_dimension=0, tiled=True).astype(jnp.float32)
    own_rows = send_start[0][:, None] + offsets[None, :]
    occupied = offsets[None, :] < run_length[0][:, None]
    pick = (occupied[:, :, None] & (own_rows[:, :, None] == rows)).astype(jnp.bfloat16)
    outgoing = jnp.dot(
        pick.reshape(-1, pack_rows), patches, preferred_element_type=jnp.float32
    ).astype(jnp.bfloat16)
    arrived = lax.all_to_all(
        outgoing.reshape(pack_count, capacity, feat_local),
        "dp",
        split_axis=0,
        concat_axis=0,
        tiled=True,
    )
    targets = (slot_start[0][:, None] + offsets[None, :]).reshape(-1)
    place = (rows[:, None] == targets[None, :]).astype(jnp.bfloat16)
    packed = jnp.dot(
        place, arrived.reshape(-1, feat_local), preferred_element_type=jnp.float32
    ).astype(jnp.bfloat16)
    head_size = query_gain.shape[0]
    heads_here = qkv_weight.shape[2] // head_size
    split_heads = projected.reshape(pack_rows, 3, heads_here, head_size)
    queries = row_norm(split_heads[:, 0], query_gain).astype(jnp.bfloat16)
    key_rows = row_norm(split_heads[:, 1], key_gain).astype(jnp.bfloat16)
    values = split_heads[:, 2].astype(jnp.bfloat16)
    scores = jnp.einsum(
        "qhd,khd->hqk", queries, key_rows, preferred_element_type=jnp.float32
    ) * head_size ** (-0.5)
    image_of = image_ids[0]
    same_image = image_of[:, None] == image_of[None, :]
    weights_raw = jnp.where(same_image[None], jnp.exp(scores), 0.0)
    totals = jnp.sum(weights_raw, axis=-1, keepdims=True)
    attention = (weights_raw / totals).astype(jnp.bfloat16)
    context = jnp.einsum(
        "hqk,khd->qhd", attention, values, preferred_element_type=jnp.float32
    ).astype(jnp.bfloat16)
    context = context.reshape(pack_rows, heads_here * head_size)
    partial_value = jnp.dot(context, out_weight, preferred_element_type=jnp.float32)
    attended = lax.psum_scatter(
        partial_value.astype(jnp.bfloat16), "mp", scatter_dimension=1, tiled=True
    )
    return (packed, attended)


def solution(mesh):
    return jax.shard_map(
        on_device,
        mesh=mesh,
        in_specs=(
            P("dp", "mp"),
            P("dp", None),
            P("dp", None),
            P("dp", None),
            P("dp", None),
            P(),
            P("dp", None, "mp"),
            P(),
            P(),
            P("mp", None),
        ),
        out_specs=(P("dp", "mp"), P("dp", "mp")),
        check_vma=False,
    )
```

profile of v0, /device:TPU:0, one launch (start us, length us, event | category | flops | bytes accessed | tf_op | source)
XLA Modules:
  0.0 220.3 jit_solution(4133471638652877734)
XLA Ops:
  7.2 0.0 all-gather.4.cloned.1.call-start
  7.2 1.2 copy.47
  8.4 0.2 convert_reduce_fusion
  8.7 13.5 %psum.7 = f32[2,128]{1,0:T(2,128)S(1)} all-reduce(f32[2,128]{1,0:T(2,128)S(1)} %pad_maximum_fusion), channel_id=1, replica_groups=mesh['dp'=8,'mp'=4] {'mp'}, use_global_device_ids=true, to_apply=%region_3.4 | all-reduce | flops 256 | bytes 2048 | tf_op jit(solution)/shard_map/psum | solution.py:36
  22.1 0.8 dynamic_slice.3
  22.9 1.0 fusion.8
  24.0 0.0 all-gather.4.cloned.1.call-update
  24.0 35.5 %all-gather.4.cloned.1.call-done = bf16[128,6144]{0,1:T(8,128)(2,1)} async-done(((bf16[128,1536]{0,1:T(8,128)(2,1)}), bf16[128,6144]{0,1:T(8,128)(2,1)}) %all-gather.4.cloned.1.call-update) | async-done | bytes 1572880 | tf_op jit(solution)/shard_map/all_gather | solution.py:41
  59.4 3.8 %all-to-all-start.1 = ((bf16[128,8,768]{0,2,1:T(8,128)(2,1)}), bf16[128,8,768]{0,2,1:T(8,128)(2,1)S(1)}, u32[]{:S(2)}, u32[]{:S(2)}) async-start(bf16[128,8,768]{0,2,1:T(8,128)(2,1)} %bitcast.83), calls=%async_computation.1 | async-start | bytes 3145728 | tf_op jit(solution)/shard_map/all_to_all | solution.py:42
  63.2 0.0 reduce-scatter.3.cloned.1.call-start
  63.3 0.0 copy-done.2
  63.3 0.0 copy-done.3
  63.3 24.0 %all-gather.1 = s32[8,3,8]{2,1,0:T(4,128)S(1)} all-gather(s32[1,3,8]{2,1,0:T(4,128)S(1)} %add_bitcast_fusion), channel_id=2, replica_groups=mesh['dp'=8,'mp'=4] {'dp'}, dimensions={0}, use_global_device_ids=true | all-gather | bytes 864 | tf_op jit(solution)/shard_map/all_gather | solution.py:44
  87.4 0.1 copy.44
  87.4 0.1 copy.46
  87.5 6.7 %copy.49 = bf16[768,3,1024]{0,2,1:T(8,128)(2,1)} copy(bf16[768,3,1024]{2,0,1:T(8,128)(2,1)} %param.16) | data formatting | bytes 9437184 | tf_op args[6]
  94.2 0.1 select_reduce_fusion
  94.3 0.0 all-to-all-done.1
  94.3 0.7 copy.48
  95.0 12.2 %convolution_convert_fusion.1 = bf16[1024,3072]{1,0:T(8,128)(2,1)} fusion(bf16[768,3072]{0,1:T(8,128)(2,1)} %bitcast.79, bf16[1024,768]{1,0:T(8,128)(2,1)S(1)} %bitcast.84, s32[1024]{0:T(1024)S(1)} %bitcast.91), kind=kOutput, calls=%fused_computation.1 | convolution fusion | flops 6447431680 | bytes 12587008 | tf_op jit(solution)/shard_map/dot_general | solution.py:51
  107.3 0.0 reduce-scatter.3.cloned.1.call-update
  107.3 0.0 reduce-scatter.5.cloned.1.call-start
  107.4 0.6 copy-done.1
  107.9 0.1 broadcast_compare_fusion
  108.0 59.1 %reduce-scatter.3.cloned.1.call-done = bf16[128,3072]{1,0:T(8,128)(2,1)} async-done(((bf16[1024,3072]{1,0:T(8,128)(2,1)}), bf16[128,3072]{1,0:T(8,128)(2,1)}) %reduce-scatter.3.cloned.1.call-update) | async-done | bytes 786448 | tf_op jit(solution)/shard_map/reduce_scatter | solution.py:56
  167.2 1.3 copy.58
  168.5 0.2 copy_convert_fusion
  168.6 0.0 copy-start.5
  168.7 0.0 copy-start.6
  168.7 0.3 slice_reduce_fusion.1
  169.0 0.3 fusion.16
  169.4 0.2 copy.57
  169.7 0.7 fusion.4
  170.4 0.3 convolution_convert_fusion.4
  170.7 7.6 %convolution_convert_fusion = bf16[128,6144]{1,0:T(8,128)(2,1)} fusion(bf16[128,1024]{0,1:T(8,128)(2,1)S(1)} %bitcast.86, bf16[1024,6144]{1,0:T(8,128)(2,1)} %param.19), kind=kOutput, calls=%fused_computation | convolution fusion | flops 1611399168 | bytes 14417920 | tf_op jit(solution)/shard_map/dot_general | solution.py:93
  178.3 0.0 reduce-scatter.5.cloned.1.call-update
  178.3 0.1 iota_add_fusion
  178.4 0.1 add.117
  178.5 0.1 iota_compare_fusion.11
  178.5 0.1 lt.37
  178.6 0.7 copy-done
  179.3 1.3 convolution_convert_fusion.2
  180.6 3.5 %all-to-all-start = ((bf16[8,32,1536]{2,1,0:T(8,128)(2,1)}), bf16[8,32,1536]{2,1,0:T(8,128)(2,1)S(1)}, u32[]{:S(2)}, u32[]{:S(2)}) async-start(bf16[8,32,1536]{2,1,0:T(8,128)(2,1)} %bitcast.3), calls=%async_computation | async-start | bytes 1572864 | tf_op jit(solution)/shard_map/all_to_all | solution.py:63
  184.1 0.1 iota_add_fusion.1
  184.2 0.1 add.111
  184.3 12.4 %all-to-all-done = bf16[8,32,1536]{2,1,0:T(8,128)(2,1)S(1)} async-done(((bf16[8,32,1536]{2,1,0:T(8,128)(2,1)}), bf16[8,32,1536]{2,1,0:T(8,128)(2,1)S(1)}, u32[]{:S(2)}, u32[]{:S(2)}) %all-to-all-start) | async-done | bytes 786464 | tf_op jit(solution)/shard_map/all_to_all | solution.py:63
  196.7 1.0 convolution_convert_fusion.3
  197.7 16.0 %reduce-scatter.5.cloned.1.call-done = bf16[128,1536]{1,0:T(8,128)(2,1)} async-done(((bf16[128,6144]{1,0:T(8,128)(2,1)}), bf16[128,1536]{1,0:T(8,128)(2,1)}) %reduce-scatter.5.cloned.1.call-update) | async-done | bytes 393232 | tf_op jit(solution)/shard_map/reduce_scatter | solution.py:94
  (18 shorter events, 0.1 us)
Async XLA Ops:
  7.2 52.3 %all-gather.4.cloned.1.call-start = ((), (), s32[]{:S(2)}) async-start(), calls=%async_computation.4 | async-start | bytes 1966080 | tf_op jit(solution)/shard_map/all_gather | solution.py:41
  59.4 3.8 %copy-start.2 = (s32[1,8]{1,0:T(1,128)S(1)}, s32[1,8]{1,0:T(1,128)}, u32[]{:S(2)}) copy-start(s32[1,8]{1,0:T(1,128)} %param.11) | copy-start | bytes 100
  59.4 3.8 %copy-start.3 = (s32[1,8]{1,0:T(1,128)S(1)}, s32[1,8]{1,0:T(1,128)}, u32[]{:S(2)}) copy-start(s32[1,8]{1,0:T(1,128)} %param.13) | copy-start | bytes 100
  59.4 3.9 %copy-start.4 = (s32[1,8]{1,0:T(1,128)S(1)}, s32[1,8]{1,0:T(1,128)}, u32[]{:S(2)}) copy-start(s32[1,8]{1,0:T(1,128)} %param.12) | copy-start | bytes 100
  59.4 34.9 %all-to-all-start.1 = ((bf16[128,8,768]{0,2,1:T(8,128)(2,1)}), bf16[128,8,768]{0,2,1:T(8,128)(2,1)S(1)}, u32[]{:S(2)}, u32[]{:S(2)}) async-start(bf16[128,8,768]{0,2,1:T(8,128)(2,1)} %bitcast.83), calls=%async_computation.1 | async-start | bytes 3145728 | tf_op jit(solution)/shard_map/all_to_all | solution.py:42
  63.2 103.9 %reduce-scatter.3.cloned.1.call-start = ((), (), s32[]{:S(2)}) async-start(), calls=%async_computation.5 | async-start | bytes 7077888 | tf_op jit(solution)/shard_map/reduce_scatter | solution.py:56
  107.3 0.7 copy-start.1
  107.3 106.4 %reduce-scatter.5.cloned.1.call-start = ((), (), s32[]{:S(2)}) async-start(), calls=%async_computation.6 | async-start | bytes 1966080 | tf_op jit(solution)/shard_map/reduce_scatter | solution.py:94
  168.6 1.0 copy-start.5
  168.7 1.0 copy-start.6
  178.3 1.0 copy-start
  180.6 16.1 %all-to-all-start = ((bf16[8,32,1536]{2,1,0:T(8,128)(2,1)}), bf16[8,32,1536]{2,1,0:T(8,128)(2,1)S(1)}, u32[]{:S(2)}, u32[]{:S(2)}) async-start(bf16[8,32,1536]{2,1,0:T(8,128)(2,1)} %bitcast.3), calls=%async_computation | async-start | bytes 1572864 | tf_op jit(solution)/shard_map/all_to_all | solution.py:63
Sparse Core Ops, SparseCore 0:
  24.1 35.2 all-gather.3
  107.4 59.6 reduce-scatter.2
  178.4 35.2 reduce-scatter.4
where the time goes:
time: 221 us; the launch traced here: 220 us
  waiting for transfers between devices  123 us (56%)
  blocking collectives  37.5 us (17%)
  matrix products  23.2 us (10%)
  between operations  13.9 us (6%)
  local copies, waits for them, and re-layouts  12.6 us (6%)
  starting transfers between devices  7.45 us (3%)
  other arithmetic  2.56 us (1%)
    reduce_scatter x1, waiting for transfers between devices, on_device(): lax.psum_scatter(partial, 'dp', scatter_dimension=0, tiled=True)  59.1 us
    all_gather x1, waiting for transfers between devices, on_device(): wide = lax.all_gather(normed, 'mp', axis=1, tiled=True)  35.5 us
    all_gather x1, blocking collectives, on_device(): tables = lax.all_gather(tables, 'dp', axis=0, tiled=True)  24 us
    reduce_scatter x1, waiting for transfers between devices, on_device(): lax.psum_scatter(partial_value.astype(jnp.bfloat16), 'mp', scatter_dimens...  16 us
    psum x1, blocking collectives, on_device(): sums = lax.psum(sums, 'mp') / (feat_local * mp_count)  13.5 us
    all_to_all x1, waiting for transfers between devices, on_device(): lax.all_to_all(outgoing.reshape(pack_count, capacity, feat_local), 'dp',...  12.4 us
    dot_general x1, matrix products, on_device(): jnp.dot(ordered, qkv_weight.reshape(qkv_weight.shape[0], local_cols), pre...  12.2 us
    unnamed x18, local copies, waits for them, and re-layouts  10.7 us
  transfers between devices with their start and end apart: 5, of which 4 were waited for; matrix products, arithmetic and copies ran while one was open for 4% of the time, Pallas kernels for 0%

commit v1 on v0

--- a/solution.py
+++ b/solution.py
@@ -39,7 +39,9 @@
     gain = lax.dynamic_slice_in_dim(norm_gain, lax.axis_index("mp") * feat_local, feat_local)
     normed = ((x - middle) * lax.rsqrt(spread + epsilon) * gain).astype(jnp.bfloat16)
     wide = lax.all_gather(normed, "mp", axis=1, tiled=True)
-    slices = lax.all_to_all(wide, "dp", split_axis=1, concat_axis=0, tiled=True)
+    slices = jnp.concatenate(
+        lax.all_to_all(jnp.stack(jnp.split(wide, lax.axis_size("dp"), axis=1)), "dp", 0, 0), axis=0
+    )
     tables = jnp.concatenate([send_start, run_length, slot_start], axis=0)[None]
     tables = lax.all_gather(tables, "dp", axis=0, tiled=True)
     starts, lengths, slots = (tables[:, 0].T, tables[:, 1].T, tables[:, 2])

time: 221 us -> 234 us (1.059)
  local copies, waits for them, and re-layouts: 12.6 us -> 23.6 us
    unnamed x18 -> x24, local copies, waits for them, and re-layouts: 10.7 us -> 20.7 us
where the time goes in v1:
time: 234 us; the launch traced here: 233 us
  waiting for transfers between devices  123 us (53%)
  blocking collectives  37.5 us (16%)
  local copies, waits for them, and re-layouts  23.6 us (10%)
  matrix products  23.2 us (10%)
  between operations  13.9 us (6%)
  starting transfers between devices  7.45 us (3%)
  other arithmetic  4.52 us (2%)
    reduce_scatter x1, waiting for transfers between devices, on_device(): lax.psum_scatter(partial, 'dp', scatter_dimension=0, tiled=True)  59.1 us
    all_gather x1, waiting for transfers between devices, on_device(): wide = lax.all_gather(normed, 'mp', axis=1, tiled=True)  35.5 us
    all_gather x1, blocking collectives, on_device(): tables = lax.all_gather(tables, 'dp', axis=0, tiled=True)  24 us
    unnamed x24, local copies, waits for them, and re-layouts  20.7 us
    reduce_scatter x1, waiting for transfers between devices, on_device(): lax.psum_scatter(partial_value.astype(jnp.bfloat16), 'mp', scatter_dimens...  16 us
    psum x1, blocking collectives, on_device(): sums = lax.psum(sums, 'mp') / (feat_local * mp_count)  13.5 us
    all_to_all x1, waiting for transfers between devices, on_device(): lax.all_to_all(outgoing.reshape(pack_count, capacity, feat_local), 'dp',...  12.4 us
    dot_general x1, matrix products, on_device(): jnp.dot(ordered, qkv_weight.reshape(qkv_weight.shape[0], local_cols), pre...  12.2 us
  transfers between devices with their start and end apart: 5, of which 4 were waited for; matrix products, arithmetic and copies ran while one was open for 4% of the time, Pallas kernels for 0%

profile of v1, /device:TPU:0, one launch (start us, length us, event | category | flops | bytes accessed | tf_op | source)
XLA Modules:
  0.0 233.2 jit_solution(4764018125740296791)
XLA Ops:
  7.2 0.0 all-gather.4.cloned.1.call-start
  7.2 1.2 convert_reduce_fusion
  8.4 13.5 %psum.7 = f32[2,128]{1,0:T(2,128)S(1)} all-reduce(f32[2,128]{1,0:T(2,128)S(1)} %pad_maximum_fusion), channel_id=1, replica_groups=mesh['dp'=8,'mp'=4] {'mp'}, use_global_device_ids=true, to_apply=%region_3.4 | all-reduce | flops 256 | bytes 2048 | tf_op jit(solution)/shard_map/psum | solution.py:36
  21.9 0.8 dynamic_slice.3
  22.7 2.0 fusion.8
  24.7 0.0 all-gather.4.cloned.1.call-update
  24.7 35.5 %all-gather.4.cloned.1.call-done = bf16[128,6144]{1,0:T(8,128)(2,1)} async-done(((bf16[128,1536]{1,0:T(8,128)(2,1)}), bf16[128,6144]{1,0:T(8,128)(2,1)}) %all-gather.4.cloned.1.call-update) | async-done | bytes 1572880 | tf_op jit(solution)/shard_map/all_gather | solution.py:41
  60.2 1.6 fusion.35
  61.8 1.6 fusion.34
  63.4 1.6 fusion.33
  65.0 1.6 fusion.32
  66.6 1.6 fusion.31
  68.2 1.6 fusion.30
  69.8 1.6 fusion.29
  71.5 1.6 fusion.28
  73.1 3.8 %all-to-all-start.1 = ((bf16[8,128,768]{2,1,0:T(8,128)(2,1)}), bf16[8,128,768]{2,1,0:T(8,128)(2,1)S(1)}, u32[]{:S(2)}, u32[]{:S(2)}) async-start(bf16[8,128,768]{2,1,0:T(8,128)(2,1)} %fusion.28), calls=%async_computation.1 | async-start | bytes 3145728 | tf_op jit(solution)/shard_map/all_to_all | solution.py:43
  76.9 0.0 reduce-scatter.3.cloned.1.call-start
  77.0 24.0 %all-gather.1 = s32[8,3,8]{2,1,0:T(4,128)S(1)} all-gather(s32[1,3,8]{2,1,0:T(4,128)S(1)} %add_bitcast_fusion), channel_id=2, replica_groups=mesh['dp'=8,'mp'=4] {'dp'}, dimensions={0}, use_global_device_ids=true | all-gather | bytes 864 | tf_op jit(solution)/shard_map/all_gather | solution.py:46
  101.0 0.1 copy.34
  101.1 0.1 copy.36
  101.1 6.7 %copy.37 = bf16[768,3,1024]{0,2,1:T(8,128)(2,1)} copy(bf16[768,3,1024]{2,0,1:T(8,128)(2,1)} %param.16) | data formatting | bytes 9437184 | tf_op args[6]
  107.9 0.1 select_reduce_fusion
  108.0 12.2 %convolution_convert_fusion.1 = bf16[1024,3072]{1,0:T(8,128)(2,1)} fusion(bf16[768,3072]{0,1:T(8,128)(2,1)} %bitcast.108, bf16[1024,768]{1,0:T(8,128)(2,1)S(1)} %bitcast.112, s32[1024]{0:T(1024)S(1)} %bitcast.119), kind=kOutput, calls=%fused_computation.1 | convolution fusion | flops 6447431680 | bytes 12587008 | tf_op jit(solution)/shard_map/dot_general | solution.py:53
  120.2 0.0 reduce-scatter.3.cloned.1.call-update
  120.2 0.0 reduce-scatter.5.cloned.1.call-start
  120.3 0.6 copy-done.1
  120.9 0.1 broadcast_compare_fusion
  121.0 59.1 %reduce-scatter.3.cloned.1.call-done = bf16[128,3072]{1,0:T(8,128)(2,1)} async-done(((bf16[1024,3072]{1,0:T(8,128)(2,1)}), bf16[128,3072]{1,0:T(8,128)(2,1)}) %reduce-scatter.3.cloned.1.call-update) | async-done | bytes 786448 | tf_op jit(solution)/shard_map/reduce_scatter | solution.py:58
  180.1 1.3 copy.46
  181.4 0.2 copy_convert_fusion
  181.6 0.3 slice_reduce_fusion.1
  181.9 0.3 fusion.16
  182.3 0.2 copy.45
  182.6 0.7 fusion.4
  183.3 0.3 convolution_convert_fusion.4
  183.6 7.6 %convolution_convert_fusion = bf16[128,6144]{1,0:T(8,128)(2,1)} fusion(bf16[128,1024]{0,1:T(8,128)(2,1)S(1)} %bitcast.114, bf16[1024,6144]{1,0:T(8,128)(2,1)} %param.19), kind=kOutput, calls=%fused_computation | convolution fusion | flops 1611399168 | bytes 14417920 | tf_op jit(solution)/shard_map/dot_general | solution.py:95
  191.2 0.1 iota_add_fusion
  191.3 0.1 add.117
  191.4 0.1 iota_compare_fusion.11
  191.5 0.1 lt.37
  191.6 0.7 copy-done
  192.2 1.3 convolution_convert_fusion.2
  193.5 3.5 %all-to-all-start = ((bf16[8,32,1536]{2,1,0:T(8,128)(2,1)}), bf16[8,32,1536]{2,1,0:T(8,128)(2,1)S(1)}, u32[]{:S(2)}, u32[]{:S(2)}) async-start(bf16[8,32,1536]{2,1,0:T(8,128)(2,1)} %bitcast.3), calls=%async_computation | async-start | bytes 1572864 | tf_op jit(solution)/shard_map/all_to_all | solution.py:65
  197.1 0.1 iota_add_fusion.1
  197.1 0.1 add.111
  197.2 12.4 %all-to-all-done = bf16[8,32,1536]{2,1,0:T(8,128)(2,1)S(1)} async-done(((bf16[8,32,1536]{2,1,0:T(8,128)(2,1)}), bf16[8,32,1536]{2,1,0:T(8,128)(2,1)S(1)}, u32[]{:S(2)}, u32[]{:S(2)}) %all-to-all-start) | async-done | bytes 786464 | tf_op jit(solution)/shard_map/all_to_all | solution.py:65
  209.6 1.0 convolution_convert_fusion.3
  210.6 16.0 %reduce-scatter.5.cloned.1.call-done = bf16[128,1536]{1,0:T(8,128)(2,1)} async-done(((bf16[128,6144]{1,0:T(8,128)(2,1)}), bf16[128,1536]{1,0:T(8,128)(2,1)}) %reduce-scatter.5.cloned.1.call-update) | async-done | bytes 393232 | tf_op jit(solution)/shard_map/reduce_scatter | solution.py:96
  (24 shorter events, 0.1 us)
Async XLA Ops:
  7.2 53.0 %all-gather.4.cloned.1.call-start = ((), (), s32[]{:S(2)}) async-start(), calls=%async_computation.4 | async-start | bytes 1966080 | tf_op jit(solution)/shard_map/all_gather | solution.py:41
  73.1 3.8 %copy-start.2 = (s32[1,8]{1,0:T(1,128)S(1)}, s32[1,8]{1,0:T(1,128)}, u32[]{:S(2)}) copy-start(s32[1,8]{1,0:T(1,128)} %param.11) | copy-start | bytes 100
  73.1 3.8 %copy-start.3 = (s32[1,8]{1,0:T(1,128)S(1)}, s32[1,8]{1,0:T(1,128)}, u32[]{:S(2)}) copy-start(s32[1,8]{1,0:T(1,128)} %param.13) | copy-start | bytes 100
  73.1 3.9 %copy-start.4 = (s32[1,8]{1,0:T(1,128)S(1)}, s32[1,8]{1,0:T(1,128)}, u32[]{:S(2)}) copy-start(s32[1,8]{1,0:T(1,128)} %param.12) | copy-start | bytes 100
  73.1 34.9 %all-to-all-start.1 = ((bf16[8,128,768]{2,1,0:T(8,128)(2,1)}), bf16[8,128,768]{2,1,0:T(8,128)(2,1)S(1)}, u32[]{:S(2)}, u32[]{:S(2)}) async-start(bf16[8,128,768]{2,1,0:T(8,128)(2,1)} %fusion.28), calls=%async_computation.1 | async-start | bytes 3145728 | tf_op jit(solution)/shard_map/all_to_all | solution.py:43
  76.9 103.2 %reduce-scatter.3.cloned.1.call-start = ((), (), s32[]{:S(2)}) async-start(), calls=%async_computation.5 | async-start | bytes 7077888 | tf_op jit(solution)/shard_map/reduce_scatter | solution.py:58
  120.2 0.7 copy-start.1
  120.2 106.4 %reduce-scatter.5.cloned.1.call-start = ((), (), s32[]{:S(2)}) async-start(), calls=%async_computation.6 | async-start | bytes 1966080 | tf_op jit(solution)/shard_map/reduce_scatter | solution.py:96
  181.6 1.0 copy-start.5
  181.6 1.0 copy-start.6
  191.2 1.0 copy-start
  193.5 16.1 %all-to-all-start = ((bf16[8,32,1536]{2,1,0:T(8,128)(2,1)}), bf16[8,32,1536]{2,1,0:T(8,128)(2,1)S(1)}, u32[]{:S(2)}, u32[]{:S(2)}) async-start(bf16[8,32,1536]{2,1,0:T(8,128)(2,1)} %bitcast.3), calls=%async_computation | async-start | bytes 1572864 | tf_op jit(solution)/shard_map/all_to_all | solution.py:65
Sparse Core Ops, SparseCore 0:
  24.8 35.2 all-gather.3
  120.4 59.6 reduce-scatter.2
  191.4 35.2 reduce-scatter.4
